TPU v7x, 256 devices: a whole 4x4x8 slice. The times are simulated.
256 devices in a mesh: tile: 4 (over y), proj: 16 (over x, z_hi, core), cuts: 4 (over z_lo).
Axes of the slice: x: 4, y: 4, z: 8 (z_hi: 2, z_lo: 4; z = z_hi * 4 + z_lo), core: 2. Of those that a mesh axis runs over, the one named last changes fastest.
Arguments:
- object_field: float32 [64, 2, 384, 2048], P(('proj', 'cuts'), None, None, 'tile'), may hold values from -5 to 5
- probe_field: float32 [2, 256, 256], replicated, may hold values from -6 to 6
- amplitudes: bfloat16 [64, 4, 6, 256, 256], P(('proj', 'cuts'), 'tile'), may hold values from 0 to 16
- pos_rows: int32 [64, 4, 6], P(('proj', 'cuts'), 'tile'), may hold values from 0 to 128
- pos_cols: int32 [64, 4, 6], P(('proj', 'cuts'), 'tile'), may hold values from 0 to 512
- counts: int32 [64, 4], P(('proj', 'cuts'), 'tile'), may hold values from 1 to 6, as said below
- admm_dual: float32 [64, 32, 2048], P(('proj', 'cuts'), None, 'tile'), may hold values from -4 to 4
- volume: float32 [32, 2048, 2048], P('cuts', ('tile', 'proj')), may hold values from -6 to 6
- proj_weights: bfloat16 [16, 2048, 2048], P(None, ('tile', 'proj')), may hold values from -0.125 to 0.125
- ray_weights: float32 [16, 2048], replicated, may hold values from -0.125 to 0.125
- angle_ids: int32 [64], replicated, may hold values from 0 to 15
Outputs:
- new_object: float32 [64, 2, 384, 2048], P(('proj', 'cuts'), None, None, 'tile')
- new_probe: float32 [2, 256, 256], replicated
- new_volume: float32 [32, 2048, 2048], P('cuts', ('tile', 'proj'))
Inputs may be any that keep to these rules, and one draw needn't show every extreme that they name: `counts`: every tile holds at least one live position and at most 6; exactly one tile of one projection holds 6, every other holds at most 3.
All inputs are finite; a program needn't handle non-finite values.
Results may differ from a plain program's by a relative error of at most 0.00095.
The roundings to bfloat16 on the way count: a program that leaves them out, or rounds other values in their place, can miss the bound.
Values may be sent and summed in bfloat16 or wider, within the bound.
A program may use at most 64 MiB of HBM per device.

v0:
```python
import math

import jax
import jax.numpy as jnp
from jax import lax
from jax.sharding import PartitionSpec as P

PB = 256


tomo_step = 1.0


def shifted(value, axis, steps):
    count = lax.axis_size(axis)
    leading, last = (max(0, -steps), min(count, count - steps))
    return lax.ppermute(value, axis, [(source, source + steps) for source in range(leading, last)])


def dft_tables(side):
    indices = jnp.arange(side, dtype=jnp.int32)
    products = indices[:, None] * indices[None, :] % side
    phase_angle = products.astype(jnp.float32) * (2.0 * math.pi / side)
    norm_factor = 1.0 / math.sqrt(side)
    return (
        (jnp.cos(phase_angle) * norm_factor).astype(jnp.bfloat16),
        (-jnp.sin(phase_angle) * norm_factor).astype(jnp.bfloat16),
    )


def matmul(left, right):
    return jnp.dot(left, right, preferred_element_type=jnp.float32)


def complex_matmul(left_real, left_imag, right_real, right_imag):
    out_real = matmul(left_real, right_real) - matmul(left_imag, right_imag)
    out_imag = matmul(left_real, right_imag) + matmul(left_imag, right_real)
    return (out_real, out_imag)


def patch_terms(patch_real, patch_imag, probe_real, probe_imag, amplitude, dft_real, dft_imag):
    wave_real = (probe_real * patch_real - probe_imag * patch_imag).astype(jnp.bfloat16)
    wave_imag = (probe_real * patch_imag + probe_imag * patch_real).astype(jnp.bfloat16)
    half_real, half_imag = complex_matmul(dft_real, dft_imag, wave_real, wave_imag)
    half_real = half_real.astype(jnp.bfloat16)
    half_imag = half_imag.astype(jnp.bfloat16)
    far_real, far_imag = complex_matmul(half_real, half_imag, dft_real, dft_imag)
    modulus = jnp.sqrt(far_real * far_real + far_imag * far_imag + 0.25)
    factor = amplitude.astype(jnp.float32) / modulus - 1.0
    diff_real = (far_real * factor).astype(jnp.bfloat16)
    diff_imag = (far_imag * factor).astype(jnp.bfloat16)
    conj_imag = -dft_imag
    back_half_real, back_half_imag = complex_matmul(dft_real, conj_imag, diff_real, diff_imag)
    back_half_real = back_half_real.astype(jnp.bfloat16)
    back_half_imag = back_half_imag.astype(jnp.bfloat16)
    back_real, back_imag = complex_matmul(back_half_real, back_half_imag, dft_real, conj_imag)
    object_real = probe_real * back_real + probe_imag * back_imag
    object_imag = probe_real * back_imag - probe_imag * back_real
    probe_grad_real = patch_real * back_real + patch_imag * back_imag
    probe_grad_imag = patch_real * back_imag - patch_imag * back_real
    energy = jnp.mean(patch_real * patch_real + patch_imag * patch_imag)
    return (
        jnp.stack([object_real, object_imag]),
        jnp.stack([probe_grad_real, probe_grad_imag]),
        energy,
    )


def tile_edges(values, offset):
    return shifted(values, "tile", offset)


def on_device(
    object_field,
    probe_field,
    amplitudes,
    pos_rows,
    pos_cols,
    counts,
    admm_dual,
    volume,
    proj_weights,
    ray_weights,
    angle_ids,
):
    half_side = PB // 2
    own_object = object_field[0]
    tile_cols = own_object.shape[2]
    from_left = tile_edges(own_object[:, :, tile_cols - half_side :], 1)
    from_right = tile_edges(own_object[:, :, :half_side], -1)
    extended = jnp.concatenate([from_left, own_object, from_right], axis=2)
    dft_real, dft_imag = dft_tables(PB)
    probe_real = probe_field[0]
    probe_imag = probe_field[1]
    zero_index = jnp.zeros((), jnp.int32)
    live_count = counts[0, 0]
    slot_total = amplitudes.shape[2]

    def slot_step(slot_index, state_tuple, weight):
        grad_sum, probe_sum, energy_sum = state_tuple
        anchor = (zero_index, pos_rows[0, 0, slot_index], pos_cols[0, 0, slot_index])
        object_patch = lax.dynamic_slice(extended, anchor, (2, PB, PB))
        object_part, probe_part, energy = patch_terms(
            object_patch[0],
            object_patch[1],
            probe_real,
            probe_imag,
            amplitudes[0, 0, slot_index],
            dft_real,
            dft_imag,
        )
        current = lax.dynamic_slice(grad_sum, anchor, (2, PB, PB))
        grad_sum = lax.dynamic_update_slice(grad_sum, current + weight * object_part, anchor)
        return (grad_sum, probe_sum + weight * probe_part, energy_sum + weight * energy)

    running = (
        jnp.zeros(extended.shape, jnp.float32),
        jnp.zeros((2, PB, PB), jnp.float32),
        jnp.zeros((), jnp.float32),
    )
    running = lax.fori_loop(
        0,
        slot_total,
        lambda slot_index, state_tuple: slot_step(
            slot_index, state_tuple, (slot_index < live_count).astype(jnp.float32)
        ),
        running,
    )
    grad_sum, probe_sum, energy_sum = running
    to_right_edge = tile_edges(grad_sum[:, :, :half_side], -1)
    to_left_edge = tile_edges(grad_sum[:, :, tile_cols + half_side :], 1)
    own_cells = grad_sum[:, :, half_side : half_side + tile_cols]
    own_cells = own_cells.at[:, :, :half_side].add(to_left_edge)
    own_cells = own_cells.at[:, :, tile_cols - half_side :].add(to_right_edge)
    probe_grad, energy = lax.psum((probe_sum, energy_sum), ("tile", "proj", "cuts"))
    new_probe = probe_field + probe_grad / (energy + 1e-05)
    probe_peak = jnp.max(probe_real * probe_real + probe_imag * probe_imag)
    new_object = (own_object + own_cells / (probe_peak + 1e-05))[None]
    slab_total = admm_dual.shape[1]
    first_row = (own_object.shape[1] - slab_total) // 2
    slab_values = new_object[:, 1, first_row : first_row + slab_total, :] + admm_dual
    arrived = lax.all_to_all(
        lax.all_to_all(slab_values, "proj", split_axis=2, concat_axis=0, tiled=True),
        "cuts",
        split_axis=1,
        concat_axis=0,
        tiled=True,
    )
    proj_count = lax.axis_size("proj")
    cuts_count = lax.axis_size("cuts")
    slab_dev = arrived.shape[1]
    u_share = arrived.shape[2]
    projections = proj_count * cuts_count
    arrived = arrived.reshape(cuts_count, proj_count, slab_dev, u_share).transpose(1, 0, 2, 3)
    target = (
        arrived.reshape(projections, slab_dev, u_share)
        .transpose(2, 0, 1)
        .reshape(u_share, projections * slab_dev)
    )
    angle_count = ray_weights.shape[0]
    x_share = volume.shape[1]
    width = volume.shape[2]
    onehot = (angle_ids[:, None] == jnp.arange(angle_count, dtype=jnp.int32)[None, :]).astype(
        jnp.float32
    )
    ray_table = jnp.dot(
        onehot, ray_weights, precision=lax.Precision.HIGHEST, preferred_element_type=jnp.float32
    )
    ray_sums = jnp.einsum("zxy,ay->azx", volume, ray_table, precision=lax.Precision.HIGHEST).astype(
        jnp.bfloat16
    )
    spread = onehot.astype(jnp.bfloat16)[:, :, None, None] * ray_sums[:, None, :, :]
    spread = spread.transpose(1, 3, 0, 2).reshape(angle_count * x_share, projections * slab_dev)
    weight_flat = proj_weights.reshape(angle_count * x_share, width)
    partial_term = lax.dot_general(
        weight_flat, spread, (((0,), (0,)), ((), ())), preferred_element_type=jnp.float32
    )
    row_start = lax.axis_index(("tile", "proj")) * u_share
    own_rows = lax.dynamic_slice_in_dim(partial_term, row_start, u_share, 0)
    partial_term = lax.dynamic_update_slice_in_dim(partial_term, own_rows - target, row_start, 0)
    summed = lax.psum(partial_term, ("tile", "proj"))
    residue = summed.astype(jnp.bfloat16)
    backproj = matmul(weight_flat, residue)
    backproj = backproj.reshape(angle_count, x_share, projections, slab_dev)
    back_sums = jnp.einsum("gxaz,ag->azx", backproj, onehot, precision=lax.Precision.HIGHEST)
    gradient = jnp.einsum("azx,ay->zxy", back_sums, ray_table, precision=lax.Precision.HIGHEST)
    new_volume = volume - tomo_step * gradient
    return (new_object, new_probe, new_volume)


def solution(mesh):
    in_specs = (
        P(("proj", "cuts"), None, None, "tile"),
        P(),
        P(("proj", "cuts"), "tile", None, None, None),
        P(("proj", "cuts"), "tile", None),
        P(("proj", "cuts"), "tile", None),
        P(("proj", "cuts"), "tile"),
        P(("proj", "cuts"), None, "tile"),
        P("cuts", ("tile", "proj"), None),
        P(None, ("tile", "proj"), None),
        P(),
        P(),
    )
    out_specs = (P(("proj", "cuts"), None, None, "tile"), P(), P("cuts", ("tile", "proj"), None))
    return jax.shard_map(
        on_device, mesh=mesh, in_specs=in_specs, out_specs=out_specs, check_vma=False
    )
```

profile of v0, /device:TPU:1, one launch (start us, length us, event | category | flops | bytes accessed | tf_op | source)
XLA Modules:
  0.0 1070.5 jit_solution(16087223290670484655)
XLA Ops:
  7.2 3.2 copy.38
  13.8 5.4 collective-permute-start
  20.5 3.4 fusion.127
  25.6 4.1 mul.437
  30.4 3.0 pad_maximum_fusion
  35.1 254.7 %while.23 = (s32[]{:T(128)}, f32[2,384,768]{1,2,0:T(8,128)}, f32[2,256,256]{2,1,0:T(8,128)}, f32[]{:T(128)}, s32[1,1,6]{2,1,0:T(1,128)S(1)}, /*index=5*/s32[1,1,...) while((s32[]{:T(128)}, f32[2,384,768]{1,2,0:T(8,128)}, ...), condition=%wide.region_2.3_spmd.clone.clone, body=%wide.region_0.2_spmd.clone.clone.sunk | while | flops 558956544 | bytes 22151564 | solution.py:121
  68.3 6.5 dynamic_update_slice.17
  110.6 6.5 dynamic_update_slice.17
  153.0 6.4 dynamic_update_slice.17
  195.4 6.6 dynamic_update_slice.17
  237.9 6.5 dynamic_update_slice.17
  280.4 6.5 dynamic_update_slice.17
  291.8 3.0 collective-permute-start.2
  296.0 4.3 fusion.138
  301.8 2.7 slice.97
  314.2 13.0 %all-to-all-start = ((f32[16,1,1024]{2,1,0:T(1,128)}), f32[16,1,1024]{2,1,0:T(1,128)S(1)}, u32[]{:S(2)}, u32[]{:S(2)}) async-start(f32[16,1,1024]{2,1,0:T(1,128)} %reshape.128), calls=%async_computation | async-start | bytes 131072 | tf_op jit(solution)/shard_map/all_to_all | solution.py:143
  327.3 79.6 %psum.22 = f32[]{:T(128)} all-reduce(f32[]{:T(128)} %get-tuple-element.384), channel_id=1, replica_groups=mesh['tile'=4,'proj'=16,'cuts'=4] {'tile','proj','cuts'}, use_global_device_ids=true, to_apply=%region_5.6 | all-reduce | flops 1 | bytes 8 | tf_op jit(solution)/shard_map/psum | solution.py:135
  409.7 3.3 all-to-all-start.1
  413.0 147.5 %all-reduce.3.cloned.1.call-done = f32[2,256,256]{2,1,0:T(8,128)} async-done(((f32[2,256,256]{2,1,0:T(8,128)}), f32[2,256,256]{2,1,0:T(8,128)}) %all-reduce.3.cloned.1.call-update) | async-done | bytes 524304 | tf_op jit(solution)/shard_map/psum | solution.py:135
  562.4 3.0 copy.48
  569.7 479.9 %all-reduce.4 = bf16[2048,512]{0,1:T(8,128)(2,1)} all-reduce(f32[2048,512]{0,1:T(8,128)} %dynamic_update_slice.13), channel_id=1, replica_groups=mesh['tile'=4,'proj'=16,'cuts'=4] {'tile','proj'}, use_global_device_ids=true, to_apply=%region_6.7 | all-reduce | flops 1048576 | bytes 6291456 | tf_op jit(solution)/shard_map/psum | solution.py:181
  1049.6 2.9 fusion.124
  1055.0 3.8 fusion.130
  1058.9 4.7 convolution_subtract_fusion.4
  (235 shorter events, 217.8 us)
Async XLA Ops:
  7.2 288.9 %copy-start = (bf16[16,32,2048]{2,1,0:T(8,128)(2,1)S(1)}, bf16[16,32,2048]{2,1,0:T(8,128)(2,1)}, u32[]{:S(2)}) copy-start(bf16[16,32,2048]{2,1,0:T(8,128)(2,1)} %param.25) | copy-start | bytes 6291460
  7.2 12.0 %copy-start.12 = (s32[64]{0:T(128)S(1)}, s32[64]{0:T(128)}, u32[]{:S(2)}) copy-start(s32[64]{0:T(128)} %param.27) | copy-start | bytes 772
  7.2 12.1 %copy-start.8 = (f32[16,2048]{1,0:T(8,128)S(1)}, f32[16,2048]{1,0:T(8,128)}, u32[]{:S(2)}) copy-start(f32[16,2048]{1,0:T(8,128)} %param.26) | copy-start | bytes 393220
  7.2 553.3 %all-reduce.3.cloned.1.call-start = ((), (), s32[]{:S(2)}) async-start(), calls=%async_computation.2 | async-start | bytes 1048576 | tf_op jit(solution)/shard_map/psum | solution.py:135
  12.5 18.0 %collective-permute-start.1 = (f32[2,384,128]{1,2,0:T(8,128)}, f32[2,384,128]{1,2,0:T(8,128)S(1)}, u32[]{:S(2)}, u32[]{:S(2)}) collective-permute-start(f32[2,384,128]{1,2,0:T(8,128)} %get-tuple-element.557), channel_id=1, source_target_pairs={{64,0},{128,64},{192,128},{65,1},{129,65},{193,129},{66,2},{130,66... | collective-permute-start | bytes 1179656 | tf_op jit(solution)/shard_map/ppermute | solution.py:17
  13.8 16.7 %collective-permute-start = (f32[2,384,128]{1,2,0:T(8,128)}, f32[2,384,128]{1,2,0:T(8,128)}, u32[]{:S(2)}, u32[]{:S(2)}) collective-permute-start(f32[2,384,128]{1,2,0:T(8,128)} %get-tuple-element.556), channel_id=1, source_target_pairs={{0,64},{64,128},{128,192},{1,65},{65,129},{129,193},{2,66},{66,130... | collective-permute-start | bytes 1179656 | tf_op jit(solution)/shard_map/ppermute | solution.py:17
  24.0 5.7 copy-start.4
  33.5 1.6 copy-start.10
  33.5 1.6 copy-start.11
  60.6 3.5 copy-start.1
  102.9 3.5 copy-start.1
  145.3 3.4 copy-start.1
  187.7 3.5 copy-start.1
  230.2 3.4 copy-start.1
  272.7 3.4 copy-start.1
  291.8 12.7 %collective-permute-start.2 = (f32[2,384,128]{1,2,0:T(8,128)}, f32[2,384,128]{1,2,0:T(8,128)}, u32[]{:S(2)}, u32[]{:S(2)}) collective-permute-start(f32[2,384,128]{1,2,0:T(8,128)} %get-tuple-element.555), channel_id=1, source_target_pairs={{0,64},{64,128},{128,192},{1,65},{65,129},{129,193},{2,66},{66,130... | collective-permute-start | bytes 1179656 | tf_op jit(solution)/shard_map/ppermute | solution.py:17
  294.7 11.8 %collective-permute-start.3 = (f32[2,384,128]{1,2,0:T(8,128)S(1)}, f32[2,384,128]{1,2,0:T(8,128)}, u32[]{:S(2)}, u32[]{:S(2)}) collective-permute-start(f32[2,384,128]{1,2,0:T(8,128)S(1)} %get-tuple-element.554), channel_id=1, source_target_pairs={{64,0},{128,64},{192,128},{65,1},{129,65},{193,129},{66,2},{130,66... | collective-permute-start | bytes 1179656 | tf_op jit(solution)/shard_map/ppermute | solution.py:17
  296.0 4.3 copy-start.9
  296.0 4.5 copy-start.5
  304.5 4.0 copy-start.2
  310.1 1.1 copy-start.3
  314.2 93.3 %all-to-all-start = ((f32[16,1,1024]{2,1,0:T(1,128)}), f32[16,1,1024]{2,1,0:T(1,128)S(1)}, u32[]{:S(2)}, u32[]{:S(2)}) async-start(f32[16,1,1024]{2,1,0:T(1,128)} %reshape.128), calls=%async_computation | async-start | bytes 131072 | tf_op jit(solution)/shard_map/all_to_all | solution.py:143
  409.7 155.7 %all-to-all-start.1 = ((f32[4,1,4096]{2,1,0:T(1,128)}), f32[4,1,4096]{2,1,0:T(1,128)S(1)}, u32[]{:S(2)}, u32[]{:S(2)}) async-start(f32[4,1,4096]{2,1,0:T(1,128)} %reshape.130), calls=%async_computation.1 | async-start | bytes 131072 | tf_op jit(solution)/shard_map/all_to_all | solution.py:142
  1055.0 4.0 copy-start.7
  (1 other events, 0.8 us)
Sparse Core Ops, SparseCore 0:
  304.6 255.8 all-reduce.2
where the time goes:
time: 1090 us; the launch traced here: 1070 us
  blocking collectives  559 us (51%)
  waiting for transfers between devices  148 us (14%)
  matrix products  141 us (13%)
  local copies, waits for them, and re-layouts  102 us (9%)
  other arithmetic  45.9 us (4%)
  loops' own time  31.6 us (3%)
  starting transfers between devices  27.2 us (2%)
  between operations  15.6 us (1%)
    psum x1, blocking collectives, on_device(): summed = lax.psum(partial_term, ('tile', 'proj'))  480 us
    psum x1, waiting for transfers between devices, on_device(): lax.psum((probe_sum, energy_sum), ('tile', 'proj', 'cuts'))  147 us
    dot_general x97, matrix products, matmul(): return jnp.dot(left, right, preferred_element_type=jnp.float32)  125 us
    psum x1, blocking collectives, on_device(): lax.psum((probe_sum, energy_sum), ('tile', 'proj', 'cuts'))  79.6 us
    dynamic_update_slice x12, local copies, waits for them, and re-layouts, slot_step(): lax.dynamic_update_slice(grad_sum, current + weight * object_part, anchor)  40.1 us
    another operation x1, loops' own time, on_device(): lax.fori_loop(0, slot_total, lambda slot_index, state_tuple: slot_step(sl...  31.6 us
  transfers between devices with their start and end apart: 7, of which 1 were waited for; matrix products, arithmetic and copies ran while one was open for 3% of the time, Pallas kernels for 0%

commit v1 on v0

--- a/solution.py
+++ b/solution.py
@@ -132,7 +132,12 @@
     own_cells = grad_sum[:, :, half_side : half_side + tile_cols]
     own_cells = own_cells.at[:, :, :half_side].add(to_left_edge)
     own_cells = own_cells.at[:, :, tile_cols - half_side :].add(to_right_edge)
-    probe_grad, energy = lax.psum((probe_sum, energy_sum), ("tile", "proj", "cuts"))
+    probe_flat = jnp.concatenate(
+        [probe_sum.reshape(-1), jnp.broadcast_to(energy_sum, (128,))]
+    )
+    probe_flat = lax.psum(probe_flat, ("tile", "proj", "cuts"))
+    probe_grad = probe_flat[: probe_sum.size].reshape(probe_sum.shape)
+    energy = probe_flat[probe_sum.size]
     new_probe = probe_field + probe_grad / (energy + 1e-05)
     probe_peak = jnp.max(probe_real * probe_real + probe_imag * probe_imag)
     new_object = (own_object + own_cells / (probe_peak + 1e-05))[None]
@@ -175,11 +180,9 @@
     partial_term = lax.dot_general(
         weight_flat, spread, (((0,), (0,)), ((), ())), preferred_element_type=jnp.float32
     )
-    row_start = lax.axis_index(("tile", "proj")) * u_share
-    own_rows = lax.dynamic_slice_in_dim(partial_term, row_start, u_share, 0)
-    partial_term = lax.dynamic_update_slice_in_dim(partial_term, own_rows - target, row_start, 0)
-    summed = lax.psum(partial_term, ("tile", "proj"))
-    residue = summed.astype(jnp.bfloat16)
+    own_rows = lax.psum_scatter(partial_term, ("tile", "proj"), scatter_dimension=0, tiled=True)
+    own_residue = (own_rows - target).astype(jnp.bfloat16)
+    residue = lax.all_gather(own_residue, ("tile", "proj"), axis=0, tiled=True)
     backproj = matmul(weight_flat, residue)
     backproj = backproj.reshape(angle_count, x_share, projections, slab_dev)
     back_sums = jnp.einsum("gxaz,ag->azx", backproj, onehot, precision=lax.Precision.HIGHEST)

time: 1090 us -> 632 us (0.58); the launches traced: 1070 us -> 629 us
  blocking collectives: 559 us -> 23.1 us
  waiting for transfers between devices: 148 us -> 256 us
  starting transfers between devices: 27.2 us -> 15 us
    psum x2 -> x0, blocking collectives: 559 us -> none  [the longest x1 480 us: on_device(): summed = lax.psum(partial_term, ('tile', 'proj'))]
    unnamed x1 -> x4, waiting for transfers between devices: 0.02 us -> 103 us
    all_to_all x0 -> x1, blocking collectives: none -> 23.1 us  [on_device(): lax.all_to_all(slab_values, 'proj', split_axis=2, concat_axis=0, tiled=True)]
    all_to_all x1 -> x0, starting transfers between devices: 13 us -> none  [on_device(): lax.all_to_all(slab_values, 'proj', split_axis=2, concat_axis=0, tiled=True)]
  transfers between devices with their start and end apart: 7 -> 8, of which waited for: 1 -> 5; matrix products, arithmetic and copies ran while one was open for 3% -> 42% of each run, Pallas kernels for 0% -> 0%
where the time goes in v1:
time: 632 us; the launch traced here: 629 us
  waiting for transfers between devices  256 us (41%)
  matrix products  143 us (23%)
  local copies, waits for them, and re-layouts  101 us (16%)
  other arithmetic  42.6 us (7%)
  loops' own time  30.5 us (5%)
  blocking collectives  23.1 us (4%)
  between operations  17.1 us (3%)
  starting transfers between devices  15 us (2%)
    psum x1, waiting for transfers between devices, on_device(): probe_flat = lax.psum(probe_flat, ('tile', 'proj', 'cuts'))  145 us
    dot_general x97, matrix products, matmul(): return jnp.dot(left, right, preferred_element_type=jnp.float32)  129 us
    unnamed x4, waiting for transfers between devices  103 us
    dynamic_update_slice x12, local copies, waits for them, and re-layouts, slot_step(): lax.dynamic_update_slice(grad_sum, current + weight * object_part, anchor)  39.9 us
    another operation x1, loops' own time, on_device(): lax.fori_loop(0, slot_total, lambda slot_index, state_tuple: slot_step(sl...  30.5 us
    all_to_all x1, blocking collectives, on_device(): lax.all_to_all(slab_values, 'proj', split_axis=2, concat_axis=0, tiled=True)  23.1 us
    unnamed x40, local copies, waits for them, and re-layouts  18.8 us
  transfers between devices with their start and end apart: 8, of which 5 were waited for; matrix products, arithmetic and copies ran while one was open for 42% of the time, Pallas kernels for 0%

profile of v1, /device:TPU:1, one launch (start us, length us, event | category | flops | bytes accessed | tf_op | source)
XLA Modules:
  0.0 628.5 jit_solution(16933225154168796481)
XLA Ops:
  8.1 3.2 copy.17
  13.5 4.0 collective-permute-start
  23.7 3.4 mul.431
  27.1 3.3 convolution_bitcast_fusion
  30.4 5.3 copy.31
  37.5 3.2 pad_maximum_fusion
  42.3 246.3 %while.23 = (s32[]{:T(128)}, f32[2,384,768]{1,2,0:T(8,128)}, f32[2,256,256]{2,1,0:T(8,128)}, f32[]{:T(128)}, s32[1,1,6]{2,1,0:T(1,128)S(1)}, /*index=5*/s32[1,1,...) while((s32[]{:T(128)}, f32[2,384,768]{1,2,0:T(8,128)}, ...), condition=%wide.region_2.3_spmd.clone.clone, body=%wide.region_0.2_spmd.clone.clone.sunk | while | flops 558956544 | bytes 21102956 | solution.py:121
  68.0 3.0 fusion.228
  75.4 6.5 %dynamic_update_slice.13 = f32[2,384,768]{1,2,0:T(8,128)} dynamic-update-slice(f32[2,384,768]{1,2,0:T(8,128)} %get-tuple-element.644, f32[2,256,256]{1,2,0:T(8,128)S(1)} %copy.50, s32[]{:T(128)} %constant.167.clone.1..sunk, s32[]{:T(128)S(6)} %select_n.153, s32[]{:T(128)S(6)} %select_n.154) | dynamic-update-slice | bytes 1048580 | tf_op jit(solution)/shard_map/while/body/eval_jaxpr/dynamic_update_slice | solution.py:113
  116.6 6.5 %dynamic_update_slice.13 = f32[2,384,768]{1,2,0:T(8,128)} dynamic-update-slice(f32[2,384,768]{1,2,0:T(8,128)} %get-tuple-element.644, f32[2,256,256]{1,2,0:T(8,128)S(1)} %copy.50, s32[]{:T(128)} %constant.167.clone.1..sunk, s32[]{:T(128)S(6)} %select_n.153, s32[]{:T(128)S(6)} %select_n.154) | dynamic-update-slice | bytes 1048580 | tf_op jit(solution)/shard_map/while/body/eval_jaxpr/dynamic_update_slice | solution.py:113
  157.9 6.6 %dynamic_update_slice.13 = f32[2,384,768]{1,2,0:T(8,128)} dynamic-update-slice(f32[2,384,768]{1,2,0:T(8,128)} %get-tuple-element.644, f32[2,256,256]{1,2,0:T(8,128)S(1)} %copy.50, s32[]{:T(128)} %constant.167.clone.1..sunk, s32[]{:T(128)S(6)} %select_n.153, s32[]{:T(128)S(6)} %select_n.154) | dynamic-update-slice | bytes 1048580 | tf_op jit(solution)/shard_map/while/body/eval_jaxpr/dynamic_update_slice | solution.py:113
  199.2 6.6 %dynamic_update_slice.13 = f32[2,384,768]{1,2,0:T(8,128)} dynamic-update-slice(f32[2,384,768]{1,2,0:T(8,128)} %get-tuple-element.644, f32[2,256,256]{1,2,0:T(8,128)S(1)} %copy.50, s32[]{:T(128)} %constant.167.clone.1..sunk, s32[]{:T(128)S(6)} %select_n.153, s32[]{:T(128)S(6)} %select_n.154) | dynamic-update-slice | bytes 1048580 | tf_op jit(solution)/shard_map/while/body/eval_jaxpr/dynamic_update_slice | solution.py:113
  240.5 6.2 dynamic_update_slice.13
  281.5 6.3 %dynamic_update_slice.13 = f32[2,384,768]{1,2,0:T(8,128)} dynamic-update-slice(f32[2,384,768]{1,2,0:T(8,128)} %get-tuple-element.644, f32[2,256,256]{1,2,0:T(8,128)S(1)} %copy.50, s32[]{:T(128)} %constant.167.clone.1..sunk, s32[]{:T(128)S(6)} %select_n.153, s32[]{:T(128)S(6)} %select_n.154) | dynamic-update-slice | bytes 1048580 | tf_op jit(solution)/shard_map/while/body/eval_jaxpr/dynamic_update_slice | solution.py:113
  290.6 5.0 collective-permute-start.2
  303.5 3.2 collective-permute-done.3
  313.2 23.1 %all_to_all.27 = f32[16,1,1024]{2,1,0:T(1,128)S(1)} all-to-all(f32[16,1,1024]{2,1,0:T(1,128)S(1)} %reshape.139), channel_id=1, replica_groups=mesh['tile'=4,'proj'=16,'cuts'=4] {'proj'}, dimensions={0} | all-to-all | bytes 131072 | tf_op jit(solution)/shard_map/all_to_all | solution.py:148
  340.0 3.3 all-to-all-start.1
  344.6 3.3 all-to-all-done.1
  348.9 102.5 %reduce-scatter.4.cloned.1.call-done = f32[32,512]{1,0:T(8,128)} async-done(((f32[2048,512]{1,0:T(8,128)}), f32[32,512]{1,0:T(8,128)}) %reduce-scatter.4.cloned.1.call-update) | async-done | bytes 65552
  453.2 145.0 %all-reduce.3.cloned.1.call-done = f32[131200]{0:T(1024)} async-done(((f32[131200]{0:T(1024)}), f32[131200]{0:T(1024)}) %all-reduce.3.cloned.1.call-update) | async-done | bytes 524816 | tf_op jit(solution)/shard_map/psum | solution.py:138
  604.0 3.0 copy.28
  612.4 3.8 fusion.126
  616.4 4.7 convolution_subtract_fusion.4
  (237 shorter events, 219.9 us)
Async XLA Ops:
  8.0 19.1 %copy-start = (bf16[16,32,2048]{2,1,0:T(8,128)(2,1)S(1)}, bf16[16,32,2048]{2,1,0:T(8,128)(2,1)}, u32[]{:S(2)}) copy-start(bf16[16,32,2048]{2,1,0:T(8,128)(2,1)} %param.25) | copy-start | bytes 6291460
  8.0 10.8 %copy-start.13 = (s32[64]{0:T(128)S(1)}, s32[64]{0:T(128)}, u32[]{:S(2)}) copy-start(s32[64]{0:T(128)} %param.27) | copy-start | bytes 772
  8.0 10.9 %copy-start.9 = (f32[16,2048]{1,0:T(8,128)S(1)}, f32[16,2048]{1,0:T(8,128)}, u32[]{:S(2)}) copy-start(f32[16,2048]{1,0:T(8,128)} %param.26) | copy-start | bytes 393220
  8.0 443.4 %reduce-scatter.4.cloned.1.call-start = ((), (), s32[]{:S(2)}) async-start(), calls=%async_computation.5 | async-start | bytes 4259840
  11.2 8.9 %copy-start.3 = (f32[8,32,2048]{2,1,0:T(8,128)S(1)}, f32[8,32,2048]{2,1,0:T(8,128)}, u32[]{:S(2)}) copy-start(f32[8,32,2048]{2,1,0:T(8,128)} %param.24) | copy-start | bytes 6291460
  13.5 24.0 %collective-permute-start = (f32[2,384,128]{1,2,0:T(8,128)}, f32[2,384,128]{1,2,0:T(8,128)S(1)}, u32[]{:S(2)}, u32[]{:S(2)}) collective-permute-start(f32[2,384,128]{1,2,0:T(8,128)} %get-tuple-element.528), channel_id=1, source_target_pairs={{0,64},{64,128},{128,192},{1,65},{65,129},{129,193},{2,66},{66,130... | collective-permute-start | bytes 1179656 | tf_op jit(solution)/shard_map/ppermute | solution.py:17
  17.6 19.9 %collective-permute-start.1 = (f32[2,384,128]{1,2,0:T(8,128)}, f32[2,384,128]{1,2,0:T(8,128)}, u32[]{:S(2)}, u32[]{:S(2)}) collective-permute-start(f32[2,384,128]{1,2,0:T(8,128)} %get-tuple-element.529), channel_id=1, source_target_pairs={{64,0},{128,64},{192,128},{65,1},{129,65},{193,129},{66,2},{130,66... | collective-permute-start | bytes 1179656 | tf_op jit(solution)/shard_map/ppermute | solution.py:17
  19.4 0.8 copy-start.7
  35.7 1.0 copy-start.5
  40.7 1.6 copy-start.11
  40.7 1.6 copy-start.12
  42.2 254.6 %copy-start.10 = (f32[1,32,512]{2,1,0:T(8,128)S(1)}, f32[1,32,512]{2,1,0:T(8,128)}, u32[]{:S(2)}) copy-start(f32[1,32,512]{2,1,0:T(8,128)} %param.23) | copy-start | bytes 196612
  288.6 8.4 %copy-start.6 = (f32[2,256,256]{2,1,0:T(8,128)S(1)}, f32[2,256,256]{2,1,0:T(8,128)}, u32[]{:S(2)}) copy-start(f32[2,256,256]{2,1,0:T(8,128)} %param.18) | copy-start | bytes 1572868
  290.6 11.8 %collective-permute-start.2 = (f32[2,384,128]{1,2,0:T(8,128)}, f32[2,384,128]{1,2,0:T(8,128)}, u32[]{:S(2)}, u32[]{:S(2)}) collective-permute-start(f32[2,384,128]{1,2,0:T(8,128)} %get-tuple-element.527), channel_id=1, source_target_pairs={{0,64},{64,128},{128,192},{1,65},{65,129},{129,193},{2,66},{66,130... | collective-permute-start | bytes 1179656 | tf_op jit(solution)/shard_map/ppermute | solution.py:17
  295.6 11.1 %collective-permute-start.3 = (f32[2,384,128]{1,2,0:T(8,128)S(1)}, f32[2,384,128]{1,2,0:T(8,128)}, u32[]{:S(2)}, u32[]{:S(2)}) collective-permute-start(f32[2,384,128]{1,2,0:T(8,128)S(1)} %get-tuple-element.526), channel_id=1, source_target_pairs={{64,0},{128,64},{192,128},{65,1},{129,65},{193,129},{66,2},{130,66... | collective-permute-start | bytes 1179656 | tf_op jit(solution)/shard_map/ppermute | solution.py:17
  298.3 9.5 %copy-start.1 = (f32[1,2,384,512]{2,3,1,0:T(8,128)S(1)}, f32[1,2,384,512]{2,3,1,0:T(8,128)}, u32[]{:S(2)}) copy-start(f32[1,2,384,512]{2,3,1,0:T(8,128)} %copy.17) | copy-start | bytes 4718596
  308.0 1.1 copy-start.4
  309.1 34.2 %copy-start.2 = (f32[2,256,256]{2,1,0:T(8,128)S(1)}, f32[2,256,256]{2,1,0:T(8,128)}, u32[]{:S(2)}) copy-start(f32[2,256,256]{2,1,0:T(8,128)} %get-tuple-element.383) | copy-start | bytes 1572868
  340.0 7.9 %all-to-all-start.1 = ((f32[4,1,4096]{2,1,0:T(1,128)}), f32[4,1,4096]{2,1,0:T(1,128)S(1)}, u32[]{:S(2)}, u32[]{:S(2)}) async-start(f32[4,1,4096]{2,1,0:T(1,128)} %reshape.141), calls=%async_computation.1 | async-start | bytes 131072 | tf_op jit(solution)/shard_map/all_to_all | solution.py:147
  343.3 254.9 %all-reduce.3.cloned.1.call-start = ((), (), s32[]{:S(2)}) async-start(), calls=%async_computation.3 | async-start | bytes 1056768 | tf_op jit(solution)/shard_map/psum | solution.py:138
  344.5 262.5 %all-gather.2.cloned.1.call-start = ((), (), s32[]{:S(2)}) async-start(), calls=%async_computation.4 | async-start | bytes 2129920 | tf_op jit(solution)/shard_map/all_gather | solution.py:185
  612.4 4.0 copy-start.8
Sparse Core Ops, SparseCore 0:
  35.8 415.5 reduce-scatter.3
  454.9 85.1 all-gather.1
Sparse Core Ops, SparseCore 1:
  349.9 248.3 all-reduce.2
